TPU v7x, 512 devices: a whole 4x4x16 slice. The times are simulated.
512 devices in a mesh: snode: 128 (over z, x, core), rhs: 4 (over y).
Axes of the slice: x: 4, y: 4, z: 16, core: 2. Of those that a mesh axis runs over, the one named last changes fastest.
Arguments:
- right_sides: float32 [3, 256, 256, 512], P(None, 'snode', None, 'rhs'), may hold values from -6 to 6
- diag_inverse: float32 [3, 256, 256, 256], P(None, 'snode', 'rhs')
- off_diagonal: bfloat16 [2, 256, 1024, 256], P(None, 'snode'), may hold values from -0.125 to 0.125
- target_snode: int32 [2, 256, 64], P(None, 'snode'), may hold values from 0 to 255, as said below
- target_block: int32 [2, 256, 64], P(None, 'snode'), may hold values from 0 to 15
Outputs:
- solution: float32 [3, 256, 256, 512], P(None, 'snode', None, 'rhs')
Inputs may be any that keep to these rules, and one draw needn't show every extreme that they name: `target_snode`: each entry is a supernode's position in the next level; the supernodes at positions i * 2 to i * 2 + 1 belong to index i of snode. Of one level's blocks held by one index of snode, at most 2 name supernodes of any one index, and some index receives exactly 2 from every index in every level.
All inputs are finite; a program needn't handle non-finite values.
Results may differ from a plain program's by a relative error of at most 0.0038.
Values may be sent and summed in bfloat16 or wider, within the bound.
No kernel may reach another device: no remote copies, remote signals or barrier semaphores. Data moves between devices by JAX's collectives and lax.ppermute only.
A program may use at most 64 MiB of HBM per device.

v0:
```python
import jax
import jax.numpy as jnp
from jax import lax
from jax.sharding import PartitionSpec as P

BR = 16


def on_device(right_sides, diag_inverse, off_diagonal, target_snode, target_block):
    precise = lax.Precision.HIGHEST
    levels = right_sides.shape[0]
    local_nodes = right_sides.shape[1]
    order_size = right_sides.shape[2]
    columns = right_sides.shape[3]
    per_node = target_snode.shape[2]
    row_blocks = order_size // BR
    devices = lax.axis_size("snode")
    outgoing = local_nodes * per_node
    capacity = 2 * outgoing // devices
    slot_count = devices * capacity
    local_rows = local_nodes * row_blocks
    front_count = 1
    front_width = columns // front_count
    full_diag = [
        lax.all_gather(diag_inverse[height], "rhs", axis=1, tiled=True) for height in range(levels)
    ]
    block_order = lax.iota(jnp.int32, outgoing)
    slot_ids = lax.iota(jnp.int32, slot_count)
    row_ids = lax.iota(jnp.int32, local_rows)
    routes = []
    for height in range(levels - 1):
        flat_target = target_snode[height].reshape(outgoing)
        owner_dev = flat_target // local_nodes
        target_code = flat_target % local_nodes * row_blocks + target_block[height].reshape(
            outgoing
        )
        earlier = (owner_dev[:, None] == owner_dev[None, :]) & (
            block_order[None, :] < block_order[:, None]
        )
        destination = owner_dev * capacity + jnp.sum(earlier.astype(jnp.int32), axis=1)
        placed = destination[None, :] == slot_ids[:, None]
        source = jnp.max(jnp.where(placed, block_order[None, :], -1), axis=1)
        slot_code = jnp.max(jnp.where(placed, target_code[None, :], -1), axis=1).reshape(
            devices, capacity
        )
        routes.append((destination, source, slot_code))
    residual_list = [right_sides[0]]
    lower_sols = [[]]
    arrivals = [[]]
    for height in range(levels):
        front = 0
        solve_result = jnp.einsum(
            "svw,swr->svr", full_diag[height], residual_list[front], precision=precise
        )
        lower_sols[front].append(solve_result)
        if height + 1 < levels:
            destination, source, slot_code = routes[height]
            update = jnp.einsum(
                "skw,swr->skr",
                off_diagonal[height],
                solve_result.astype(jnp.bfloat16),
                preferred_element_type=jnp.float32,
            )
            update = update.astype(jnp.bfloat16).reshape(outgoing, BR * front_width)
            outbound = jnp.where(
                (source >= 0)[:, None], update[jnp.maximum(source, 0)], jnp.zeros((), jnp.bfloat16)
            )
            outbound = outbound.reshape(devices, capacity, BR * front_width)
            inbound, inbound_code = (
                lax.all_to_all(outbound, "snode", split_axis=0, concat_axis=0, tiled=True),
                lax.all_to_all(slot_code, "snode", split_axis=0, concat_axis=0, tiled=True),
            )
            arrived = inbound_code.reshape(slot_count)
            arrivals[front].append(arrived)
            gather_table = (arrived[None, :] == row_ids[:, None]).astype(jnp.bfloat16)
            summed = jnp.dot(
                gather_table,
                inbound.reshape(slot_count, BR * front_width),
                preferred_element_type=jnp.float32,
            )
            summed = summed.reshape(local_nodes, order_size, front_width)
            upcoming = right_sides[height + 1]
            residual_list[front] = upcoming - summed
    answer = [[None] * levels]
    for height in range(levels - 1, -1, -1):
        front = 0
        if height == levels - 1:
            carried = lower_sols[front][height]
        else:
            destination, source, slot_code = routes[height]
            above_rows = (
                answer[front][height + 1].astype(jnp.bfloat16).reshape(local_rows, BR * front_width)
            )
            arrived = arrivals[front][height]
            outbound = jnp.where(
                (arrived >= 0)[:, None],
                above_rows[jnp.maximum(arrived, 0)],
                jnp.zeros((), jnp.bfloat16),
            )
            outbound = outbound.reshape(devices, capacity, BR * front_width)
            returned = lax.all_to_all(outbound, "snode", split_axis=0, concat_axis=0, tiled=True)
            block_rows = returned.reshape(slot_count, BR * front_width)[destination]
            block_rows = block_rows.reshape(local_nodes, per_node * BR, front_width)
            carried = lower_sols[front][height] - jnp.einsum(
                "skw,skr->swr", off_diagonal[height], block_rows, preferred_element_type=jnp.float32
            )
        result = jnp.einsum("swv,swr->svr", full_diag[height], carried, precision=precise)
        answer[front][height] = result
    stacked = [answer[0][height] for height in range(levels)]
    return jnp.stack(stacked, axis=0)


def solution(mesh):
    in_specs = (
        P(None, "snode", None, "rhs"),
        P(None, "snode", "rhs", None),
        P(None, "snode", None, None),
        P(None, "snode", None),
        P(None, "snode", None),
    )
    out_specs = P(None, "snode", None, "rhs")
    return jax.shard_map(
        on_device, mesh=mesh, in_specs=in_specs, out_specs=out_specs, check_vma=False
    )
```

profile of v0, /device:TPU:41, one launch (start us, length us, event | category | flops | bytes accessed | tf_op | source)
XLA Modules:
  0.0 373.4 jit_solution(11072806632343055890)
XLA Ops:
  2.8 19.3 %all-to-all-start = ((s32[128,1,2]{2,1,0:T(1,128)}), s32[128,1,2]{2,1,0:T(1,128)S(1)}, u32[]{:S(2)}, u32[]{:S(2)}) async-start(s32[128,1,2]{2,1,0:T(1,128)} %bitcast.2), calls=%async_computation | async-start | bytes 131072 | tf_op jit(solution)/shard_map/all_to_all | solution.py:71
  23.9 11.0 %all-gather = f32[1,2,256,256]{3,2,1,0:T(8,128)S(1)} all-gather(f32[1,2,64,256]{3,2,1,0:T(8,128)S(1)} %get-tuple-element.13), channel_id=2, replica_groups=mesh['snode'=128,'rhs'=4] {'rhs'}, dimensions={2}, use_global_device_ids=true | all-gather | bytes 655360 | tf_op jit(solution)/shard_map/all_gather | solution.py:25
  40.5 2.3 gather_fusion
  42.8 1.7 gather.27
  45.5 18.8 %all-to-all-start.2 = ((s32[128,1,2]{2,1,0:T(1,128)}), s32[128,1,2]{2,1,0:T(1,128)S(1)}, u32[]{:S(2)}, u32[]{:S(2)}) async-start(s32[128,1,2]{2,1,0:T(1,128)} %bitcast.8), calls=%async_computation.2 | async-start | bytes 131072 | tf_op jit(solution)/shard_map/all_to_all | solution.py:71
  64.3 2.0 broadcast_select_fusion.2
  66.3 12.2 %all-to-all-done.2 = s32[128,1,2]{2,1,0:T(1,128)S(1)} async-done(((s32[128,1,2]{2,1,0:T(1,128)}), s32[128,1,2]{2,1,0:T(1,128)S(1)}, u32[]{:S(2)}, u32[]{:S(2)}) %all-to-all-start.2) | async-done | bytes 1056 | tf_op jit(solution)/shard_map/all_to_all | solution.py:71
  78.4 7.5 %all-to-all-start.1 = ((bf16[128,2,2048]{2,1,0:T(2,128)(2,1)}), bf16[128,2,2048]{2,1,0:T(2,128)(2,1)}, u32[]{:S(2)}, u32[]{:S(2)}) async-start(bf16[128,2,2048]{2,1,0:T(2,128)(2,1)} %broadcast_select_fusion.2), calls=%async_computation.1 | async-start | bytes 2097152 | tf_op jit(solution)/shard_map/all_to_all | solution.py:70
  86.7 11.3 %all-gather.1 = f32[1,2,256,256]{3,2,1,0:T(8,128)S(1)} all-gather(f32[1,2,64,256]{3,2,1,0:T(8,128)S(1)} %get-tuple-element.15), channel_id=3, replica_groups=mesh['snode'=128,'rhs'=4] {'rhs'}, dimensions={2}, use_global_device_ids=true | all-gather | bytes 655360 | tf_op jit(solution)/shard_map/all_gather | solution.py:25
  98.5 1.9 maximum_reduce_fusion
  100.6 40.6 %all-to-all-done.1 = bf16[128,2,2048]{2,1,0:T(2,128)(2,1)} async-done(((bf16[128,2,2048]{2,1,0:T(2,128)(2,1)}), bf16[128,2,2048]{2,1,0:T(2,128)(2,1)}, u32[]{:S(2)}, u32[]{:S(2)}) %all-to-all-start.1) | async-done | bytes 1048608 | tf_op jit(solution)/shard_map/all_to_all | solution.py:70
  141.2 2.3 reshape.483
  147.7 2.5 gather_fusion.1
  151.9 2.0 broadcast_select_fusion
  154.0 7.0 %all-to-all-start.3 = ((bf16[128,2,2048]{2,1,0:T(2,128)(2,1)}), bf16[128,2,2048]{2,1,0:T(2,128)(2,1)}, u32[]{:S(2)}, u32[]{:S(2)}) async-start(bf16[128,2,2048]{2,1,0:T(2,128)(2,1)} %broadcast_select_fusion), calls=%async_computation.3 | async-start | bytes 2097152 | tf_op jit(solution)/shard_map/all_to_all | solution.py:70
  161.0 11.1 %all-gather.2 = f32[1,2,256,256]{3,2,1,0:T(8,128)S(1)} all-gather(f32[1,2,64,256]{3,2,1,0:T(8,128)S(1)} %copy-done.11), channel_id=4, replica_groups=mesh['snode'=128,'rhs'=4] {'rhs'}, dimensions={2}, use_global_device_ids=true | all-gather | bytes 655360 | tf_op jit(solution)/shard_map/all_gather | solution.py:25
  173.3 42.9 %all-to-all-done.3 = bf16[128,2,2048]{2,1,0:T(2,128)(2,1)} async-done(((bf16[128,2,2048]{2,1,0:T(2,128)(2,1)}), bf16[128,2,2048]{2,1,0:T(2,128)(2,1)}, u32[]{:S(2)}, u32[]{:S(2)}) %all-to-all-start.3) | async-done | bytes 1048608 | tf_op jit(solution)/shard_map/all_to_all | solution.py:70
  216.2 2.3 reshape.486
  226.0 3.3 broadcast_select_fusion.1
  229.3 7.2 %all-to-all-start.4 = ((bf16[128,2,2048]{2,1,0:T(2,128)(2,1)}), bf16[128,2,2048]{2,1,0:T(2,128)(2,1)}, u32[]{:S(2)}, u32[]{:S(2)}) async-start(bf16[128,2,2048]{2,1,0:T(2,128)(2,1)} %broadcast_select_fusion.1), calls=%async_computation.4 | async-start | bytes 2097152 | tf_op jit(solution)/shard_map/all_to_all | solution.py:101
  237.7 54.0 %all-to-all-done.4 = bf16[128,2,2048]{2,1,0:T(2,128)(2,1)} async-done(((bf16[128,2,2048]{2,1,0:T(2,128)(2,1)}), bf16[128,2,2048]{2,1,0:T(2,128)(2,1)}, u32[]{:S(2)}, u32[]{:S(2)}) %all-to-all-start.4) | async-done | bytes 1048608 | tf_op jit(solution)/shard_map/all_to_all | solution.py:101
  301.0 3.2 broadcast_select_fusion.3
  304.2 7.0 %all-to-all-start.5 = ((bf16[128,2,2048]{2,1,0:T(2,128)(2,1)}), bf16[128,2,2048]{2,1,0:T(2,128)(2,1)}, u32[]{:S(2)}, u32[]{:S(2)}) async-start(bf16[128,2,2048]{2,1,0:T(2,128)(2,1)} %broadcast_select_fusion.3), calls=%async_computation.5 | async-start | bytes 2097152 | tf_op jit(solution)/shard_map/all_to_all | solution.py:101
  311.3 55.1 %all-to-all-done.5 = bf16[128,2,2048]{2,1,0:T(2,128)(2,1)} async-done(((bf16[128,2,2048]{2,1,0:T(2,128)(2,1)}), bf16[128,2,2048]{2,1,0:T(2,128)(2,1)}, u32[]{:S(2)}, u32[]{:S(2)}) %all-to-all-start.5) | async-done | bytes 1048608 | tf_op jit(solution)/shard_map/all_to_all | solution.py:101
  (126 shorter events, 44.5 us)
Async XLA Ops:
  0.0 37.5 %copy-start = (bf16[2,2,1024,256]{3,2,1,0:T(8,128)(2,1)S(1)}, bf16[2,2,1024,256]{3,2,1,0:T(8,128)(2,1)}, u32[]{:S(2)}) copy-start(bf16[2,2,1024,256]{3,2,1,0:T(8,128)(2,1)} %param.7) | copy-start | bytes 6291460
  0.9 37.1 %copy-start.17 = (s32[1,2,64]{2,1,0:T(2,128)}, s32[1,2,64]{2,1,0:T(2,128)S(1)}, u32[]{:S(2)}) copy-start(s32[1,2,64]{2,1,0:T(2,128)S(1)} %get-tuple-element.16) | copy-start | bytes 1540
  1.9 22.0 %copy-start.19 = (s32[128]{0:T(128)}, s32[128]{0:T(128)S(1)}, u32[]{:S(2)}) copy-start(s32[128]{0:T(128)S(1)} %convert_reduce_fusion.1) | copy-start | bytes 1540
  2.8 42.6 %all-to-all-start = ((s32[128,1,2]{2,1,0:T(1,128)}), s32[128,1,2]{2,1,0:T(1,128)S(1)}, u32[]{:S(2)}, u32[]{:S(2)}) async-start(s32[128,1,2]{2,1,0:T(1,128)} %bitcast.2), calls=%async_computation | async-start | bytes 131072 | tf_op jit(solution)/shard_map/all_to_all | solution.py:71
  34.9 3.3 copy-start.1
  35.2 5.2 %copy-start.21 = (s32[128]{0:T(128)}, s32[128]{0:T(128)S(1)}, u32[]{:S(2)}) copy-start(s32[128]{0:T(128)S(1)} %convert_reduce_fusion) | copy-start | bytes 1540
  45.5 53.0 %copy-start.9 = (s32[128,1,2]{2,1,0:T(1,128)}, s32[128,1,2]{2,1,0:T(1,128)S(1)}, u32[]{:S(2)}) copy-start(s32[128,1,2]{2,1,0:T(1,128)S(1)} %all-to-all-done) | copy-start | bytes 3076
  45.5 32.9 %all-to-all-start.2 = ((s32[128,1,2]{2,1,0:T(1,128)}), s32[128,1,2]{2,1,0:T(1,128)S(1)}, u32[]{:S(2)}, u32[]{:S(2)}) async-start(s32[128,1,2]{2,1,0:T(1,128)} %bitcast.8), calls=%async_computation.2 | async-start | bytes 131072 | tf_op jit(solution)/shard_map/all_to_all | solution.py:71
  78.4 62.8 %all-to-all-start.1 = ((bf16[128,2,2048]{2,1,0:T(2,128)(2,1)}), bf16[128,2,2048]{2,1,0:T(2,128)(2,1)}, u32[]{:S(2)}, u32[]{:S(2)}) async-start(bf16[128,2,2048]{2,1,0:T(2,128)(2,1)} %broadcast_select_fusion.2), calls=%async_computation.1 | async-start | bytes 2097152 | tf_op jit(solution)/shard_map/all_to_all | solution.py:70
  98.0 47.1 %copy-start.3 = (f32[1,2,256,256]{3,2,1,0:T(8,128)}, f32[1,2,256,256]{3,2,1,0:T(8,128)S(1)}, u32[]{:S(2)}) copy-start(f32[1,2,256,256]{3,2,1,0:T(8,128)S(1)} %all-gather.1) | copy-start | bytes 1572868
  151.9 20.3 %copy-start.13 = (s32[128,2]{1,0:T(8,128)S(1)}, s32[128,2]{1,0:T(8,128)}, u32[]{:S(2)}) copy-start(s32[128,2]{1,0:T(8,128)} %get-tuple-element.29) | copy-start | bytes 3076
  154.0 7.0 %copy-start.11 = (f32[1,2,64,256]{3,2,1,0:T(8,128)S(1)}, f32[1,2,64,256]{3,2,1,0:T(8,128)}, u32[]{:S(2)}) copy-start(f32[1,2,64,256]{3,2,1,0:T(8,128)} %get-tuple-element.14) | copy-start | bytes 393220
  154.0 18.1 %copy-start.14 = (s32[128,2]{1,0:T(8,128)S(1)}, s32[128,2]{1,0:T(8,128)}, u32[]{:S(2)}) copy-start(s32[128,2]{1,0:T(8,128)} %get-tuple-element.28) | copy-start | bytes 3076
  154.0 62.2 %all-to-all-start.3 = ((bf16[128,2,2048]{2,1,0:T(2,128)(2,1)}), bf16[128,2,2048]{2,1,0:T(2,128)(2,1)}, u32[]{:S(2)}, u32[]{:S(2)}) async-start(bf16[128,2,2048]{2,1,0:T(2,128)(2,1)} %broadcast_select_fusion), calls=%async_computation.3 | async-start | bytes 2097152 | tf_op jit(solution)/shard_map/all_to_all | solution.py:70
  226.0 10.5 %copy-start.18 = (s32[1,2,64]{2,1,0:T(2,128)S(1)}, s32[1,2,64]{2,1,0:T(2,128)}, u32[]{:S(2)}) copy-start(s32[1,2,64]{2,1,0:T(2,128)} %copy-done.17) | copy-start | bytes 1540
  226.0 10.5 %copy-start.22 = (s32[128]{0:T(128)S(1)}, s32[128]{0:T(128)}, u32[]{:S(2)}) copy-start(s32[128]{0:T(128)} %copy-done.21) | copy-start | bytes 1540
  226.0 10.6 %copy-start.12 = (s32[128,2]{1,0:T(8,128)S(1)}, s32[128,2]{1,0:T(8,128)}, u32[]{:S(2)}) copy-start(s32[128,2]{1,0:T(8,128)} %get-tuple-element.5) | copy-start | bytes 3076
  226.0 10.7 %copy-start.10 = (s32[128,1,2]{2,1,0:T(1,128)S(1)}, s32[128,1,2]{2,1,0:T(1,128)}, u32[]{:S(2)}) copy-start(s32[128,1,2]{2,1,0:T(1,128)} %copy-done.9) | copy-start | bytes 3076
  229.3 62.4 %all-to-all-start.4 = ((bf16[128,2,2048]{2,1,0:T(2,128)(2,1)}), bf16[128,2,2048]{2,1,0:T(2,128)(2,1)}, u32[]{:S(2)}, u32[]{:S(2)}) async-start(bf16[128,2,2048]{2,1,0:T(2,128)(2,1)} %broadcast_select_fusion.1), calls=%async_computation.4 | async-start | bytes 2097152 | tf_op jit(solution)/shard_map/all_to_all | solution.py:101
  301.0 10.2 %copy-start.16 = (s32[1,2,64]{2,1,0:T(2,128)S(1)}, s32[1,2,64]{2,1,0:T(2,128)}, u32[]{:S(2)}) copy-start(s32[1,2,64]{2,1,0:T(2,128)} %copy-done.15) | copy-start | bytes 1540
  301.0 10.3 %copy-start.20 = (s32[128]{0:T(128)S(1)}, s32[128]{0:T(128)}, u32[]{:S(2)}) copy-start(s32[128]{0:T(128)} %copy-done.19) | copy-start | bytes 1540
  304.2 62.2 %all-to-all-start.5 = ((bf16[128,2,2048]{2,1,0:T(2,128)(2,1)}), bf16[128,2,2048]{2,1,0:T(2,128)(2,1)}, u32[]{:S(2)}, u32[]{:S(2)}) async-start(bf16[128,2,2048]{2,1,0:T(2,128)(2,1)} %broadcast_select_fusion.3), calls=%async_computation.5 | async-start | bytes 2097152 | tf_op jit(solution)/shard_map/all_to_all | solution.py:101
  367.8 3.1 copy-start.6
  369.6 1.9 copy-start.2
  (5 other events, 5.9 us)
where the time goes:
time: 374 us; the launch traced here: 373 us
  waiting for transfers between devices  205 us (55%)
  starting transfers between devices  66.6 us (18%)
  local copies, waits for them, and re-layouts  40.2 us (11%)
  blocking collectives  33.4 us (9%)
  other arithmetic  15.2 us (4%)
  matrix products  12.6 us (3%)
    all_to_all x4, waiting for transfers between devices, on_device(): lax.all_to_all(outbound, 'snode', split_axis=0, concat_axis=0, tiled=True)  193 us
    all_to_all x2, starting transfers between devices, on_device(): lax.all_to_all(slot_code, 'snode', split_axis=0, concat_axis=0, tiled=True)  38 us
    all_gather x3, blocking collectives, on_device(): lax.all_gather(diag_inverse[height], 'rhs', axis=1, tiled=True)  33.4 us
    all_to_all x4, starting transfers between devices, on_device(): lax.all_to_all(outbound, 'snode', split_axis=0, concat_axis=0, tiled=True)  28.6 us
    all_to_all x2, waiting for transfers between devices, on_device(): lax.all_to_all(slot_code, 'snode', split_axis=0, concat_axis=0, tiled=True)  12.2 us
    gather x4, local copies, waits for them, and re-layouts, on_device(): update[jnp.maximum(source, 0)]  8.3 us
  transfers between devices with their start and end apart: 6, of which 5 were waited for; matrix products, arithmetic and copies ran while one was open for 5% of the time, Pallas kernels for 0%

commit v1 on v0

--- a/solution.py
+++ b/solution.py
@@ -4,6 +4,13 @@
 from jax.sharding import PartitionSpec as P
 
 BR = 16
+
+
+def exchange_gather(x, axis, along):
+    size = lax.axis_size(axis)
+    pieces = jnp.stack([x for _ in range(size)])
+    pieces = lax.all_to_all(pieces, axis, split_axis=0, concat_axis=0)
+    return jnp.concatenate(pieces, axis=along)
 
 
 def on_device(right_sides, diag_inverse, off_diagonal, target_snode, target_block):
@@ -21,9 +28,7 @@
     local_rows = local_nodes * row_blocks
     front_count = 1
     front_width = columns // front_count
-    full_diag = [
-        lax.all_gather(diag_inverse[height], "rhs", axis=1, tiled=True) for height in range(levels)
-    ]
+    full_diag = [exchange_gather(diag_inverse[height], "rhs", 1) for height in range(levels)]
     block_order = lax.iota(jnp.int32, outgoing)
     slot_ids = lax.iota(jnp.int32, slot_count)
     row_ids = lax.iota(jnp.int32, local_rows)

time: 374 us -> 387 us (1.035)
  waiting for transfers between devices: 205 us -> 243 us
  blocking collectives: 33.4 us -> 0 us
  starting transfers between devices: 66.6 us -> 72 us
    all_gather x3 -> x0, blocking collectives: 33.4 us -> none  [on_device(): lax.all_gather(diag_inverse[height], 'rhs', axis=1, tiled=True)]
    all_to_all x4, waiting for transfers between devices: 193 us -> 213 us  [on_device(): lax.all_to_all(outbound, 'snode', split_axis=0, concat_axis=0, tiled=True)]
    all_to_all x0 -> x3, starting transfers between devices: none -> 15.1 us  [exchange_gather(): pieces = lax.all_to_all(pieces, axis, split_axis=0, concat_axis=0)]
    all_to_all x2, starting transfers between devices: 38 us -> 27 us  [on_device(): lax.all_to_all(slot_code, 'snode', split_axis=0, concat_axis=0, tiled=True)]
    all_to_all x2, waiting for transfers between devices: 12.2 us -> 20.8 us  [on_device(): lax.all_to_all(slot_code, 'snode', split_axis=0, concat_axis=0, tiled=True)]
    all_to_all x0 -> x3, waiting for transfers between devices: none -> 8.3 us  [exchange_gather(): pieces = lax.all_to_all(pieces, axis, split_axis=0, concat_axis=0)]
  transfers between devices with their start and end apart: 6 -> 9, of which waited for: 5 -> 8; matrix products, arithmetic and copies ran while one was open for 5% -> 8% of each run, Pallas kernels for 0% -> 0%
where the time goes in v1:
time: 387 us; the launch traced here: 386 us
  waiting for transfers between devices  243 us (63%)
  starting transfers between devices  72 us (19%)
  local copies, waits for them, and re-layouts  42.7 us (11%)
  other arithmetic  15.6 us (4%)
  matrix products  12.7 us (3%)
    all_to_all x4, waiting for transfers between devices, on_device(): lax.all_to_all(outbound, 'snode', split_axis=0, concat_axis=0, tiled=True)  213 us
    all_to_all x4, starting transfers between devices, on_device(): lax.all_to_all(outbound, 'snode', split_axis=0, concat_axis=0, tiled=True)  29.9 us
    all_to_all x2, starting transfers between devices, on_device(): lax.all_to_all(slot_code, 'snode', split_axis=0, concat_axis=0, tiled=True)  27 us
    all_to_all x2, waiting for transfers between devices, on_device(): lax.all_to_all(slot_code, 'snode', split_axis=0, concat_axis=0, tiled=True)  20.8 us
    all_to_all x3, starting transfers between devices, exchange_gather(): pieces = lax.all_to_all(pieces, axis, split_axis=0, concat_axis=0)  15.1 us
    gather x4, local copies, waits for them, and re-layouts, on_device(): update[jnp.maximum(source, 0)]  8.41 us
    all_to_all x3, waiting for transfers between devices, exchange_gather(): pieces = lax.all_to_all(pieces, axis, split_axis=0, concat_axis=0)  8.3 us
  transfers between devices with their start and end apart: 9, of which 8 were waited for; matrix products, arithmetic and copies ran while one was open for 8% of the time, Pallas kernels for 0%

profile of v1, /device:TPU:41, one launch (start us, length us, event | category | flops | bytes accessed | tf_op | source)
XLA Modules:
  0.0 386.1 jit_solution(8707590542152738874)
XLA Ops:
  2.6 4.3 %all-to-all-start = ((f32[4,2,64,256]{3,2,1,0:T(8,128)}), f32[4,2,64,256]{3,2,1,0:T(8,128)S(1)}, u32[]{:S(2)}, u32[]{:S(2)}) async-start(f32[4,2,64,256]{3,2,1,0:T(8,128)} %stack.21), calls=%async_computation | async-start | bytes 1048576 | tf_op jit(solution)/shard_map/all_to_all | solution.py:12
  11.8 2.3 all-to-all-done
  14.1 20.7 %all-to-all-start.1 = ((s32[128,1,2]{2,1,0:T(1,128)}), s32[128,1,2]{2,1,0:T(1,128)S(1)}, u32[]{:S(2)}, u32[]{:S(2)}) async-start(s32[128,1,2]{2,1,0:T(1,128)} %bitcast.4), calls=%async_computation.1 | async-start | bytes 131072 | tf_op jit(solution)/shard_map/all_to_all | solution.py:76
  37.3 11.8 %all-to-all-done.1 = s32[128,1,2]{2,1,0:T(1,128)S(1)} async-done(((s32[128,1,2]{2,1,0:T(1,128)}), s32[128,1,2]{2,1,0:T(1,128)S(1)}, u32[]{:S(2)}, u32[]{:S(2)}) %all-to-all-start.1) | async-done | bytes 1056 | tf_op jit(solution)/shard_map/all_to_all | solution.py:76
  49.1 6.3 %all-to-all-start.4 = ((s32[128,1,2]{2,1,0:T(1,128)}), s32[128,1,2]{2,1,0:T(1,128)S(1)}, u32[]{:S(2)}, u32[]{:S(2)}) async-start(s32[128,1,2]{2,1,0:T(1,128)} %bitcast.12), calls=%async_computation.4 | async-start | bytes 131072 | tf_op jit(solution)/shard_map/all_to_all | solution.py:76
  56.5 2.5 gather_fusion
  60.8 9.0 %all-to-all-done.4 = s32[128,1,2]{2,1,0:T(1,128)S(1)} async-done(((s32[128,1,2]{2,1,0:T(1,128)}), s32[128,1,2]{2,1,0:T(1,128)S(1)}, u32[]{:S(2)}, u32[]{:S(2)}) %all-to-all-start.4) | async-done | bytes 1056 | tf_op jit(solution)/shard_map/all_to_all | solution.py:76
  70.6 5.3 %all-to-all-start.3 = ((f32[4,2,64,256]{3,2,1,0:T(8,128)}), f32[4,2,64,256]{3,2,1,0:T(8,128)}, u32[]{:S(2)}, u32[]{:S(2)}) async-start(f32[4,2,64,256]{3,2,1,0:T(8,128)} %stack.22), calls=%async_computation.3 | async-start | bytes 1048576 | tf_op jit(solution)/shard_map/all_to_all | solution.py:12
  77.9 6.0 %all-to-all-done.3 = f32[4,2,64,256]{3,2,1,0:T(8,128)} async-done(((f32[4,2,64,256]{3,2,1,0:T(8,128)}), f32[4,2,64,256]{3,2,1,0:T(8,128)}, u32[]{:S(2)}, u32[]{:S(2)}) %all-to-all-start.3) | async-done | bytes 524320 | tf_op jit(solution)/shard_map/all_to_all | solution.py:12
  83.9 8.6 %all-to-all-start.2 = ((bf16[128,2,2048]{2,1,0:T(2,128)(2,1)}), bf16[128,2,2048]{2,1,0:T(2,128)(2,1)}, u32[]{:S(2)}, u32[]{:S(2)}) async-start(bf16[128,2,2048]{2,1,0:T(2,128)(2,1)} %broadcast_select_fusion.2), calls=%async_computation.2 | async-start | bytes 2097152 | tf_op jit(solution)/shard_map/all_to_all | solution.py:75
  96.4 51.4 %all-to-all-done.2 = bf16[128,2,2048]{2,1,0:T(2,128)(2,1)} async-done(((bf16[128,2,2048]{2,1,0:T(2,128)(2,1)}), bf16[128,2,2048]{2,1,0:T(2,128)(2,1)}, u32[]{:S(2)}, u32[]{:S(2)}) %all-to-all-start.2) | async-done | bytes 1048608 | tf_op jit(solution)/shard_map/all_to_all | solution.py:75
  148.6 5.5 %all-to-all-start.6 = ((f32[4,2,64,256]{3,2,1,0:T(8,128)}), f32[4,2,64,256]{3,2,1,0:T(8,128)}, u32[]{:S(2)}, u32[]{:S(2)}) async-start(f32[4,2,64,256]{3,2,1,0:T(8,128)} %stack.23), calls=%async_computation.6 | async-start | bytes 1048576 | tf_op jit(solution)/shard_map/all_to_all | solution.py:12
  154.0 2.2 reshape.506
  160.5 2.4 gather_fusion.1
  164.7 2.0 broadcast_select_fusion
  166.7 7.4 %all-to-all-start.5 = ((bf16[128,2,2048]{2,1,0:T(2,128)(2,1)}), bf16[128,2,2048]{2,1,0:T(2,128)(2,1)}, u32[]{:S(2)}, u32[]{:S(2)}) async-start(bf16[128,2,2048]{2,1,0:T(2,128)(2,1)} %broadcast_select_fusion), calls=%async_computation.5 | async-start | bytes 2097152 | tf_op jit(solution)/shard_map/all_to_all | solution.py:75
  176.3 52.9 %all-to-all-done.5 = bf16[128,2,2048]{2,1,0:T(2,128)(2,1)} async-done(((bf16[128,2,2048]{2,1,0:T(2,128)(2,1)}), bf16[128,2,2048]{2,1,0:T(2,128)(2,1)}, u32[]{:S(2)}, u32[]{:S(2)}) %all-to-all-start.5) | async-done | bytes 1048608 | tf_op jit(solution)/shard_map/all_to_all | solution.py:75
  229.2 2.2 reshape.511
  239.1 3.2 broadcast_select_fusion.1
  242.3 7.0 %all-to-all-start.7 = ((bf16[128,2,2048]{2,1,0:T(2,128)(2,1)}), bf16[128,2,2048]{2,1,0:T(2,128)(2,1)}, u32[]{:S(2)}, u32[]{:S(2)}) async-start(bf16[128,2,2048]{2,1,0:T(2,128)(2,1)} %broadcast_select_fusion.1), calls=%async_computation.7 | async-start | bytes 2097152 | tf_op jit(solution)/shard_map/all_to_all | solution.py:106
  250.5 54.0 %all-to-all-done.7 = bf16[128,2,2048]{2,1,0:T(2,128)(2,1)} async-done(((bf16[128,2,2048]{2,1,0:T(2,128)(2,1)}), bf16[128,2,2048]{2,1,0:T(2,128)(2,1)}, u32[]{:S(2)}, u32[]{:S(2)}) %all-to-all-start.7) | async-done | bytes 1048608 | tf_op jit(solution)/shard_map/all_to_all | solution.py:106
  313.8 3.2 broadcast_select_fusion.3
  317.0 7.0 %all-to-all-start.8 = ((bf16[128,2,2048]{2,1,0:T(2,128)(2,1)}), bf16[128,2,2048]{2,1,0:T(2,128)(2,1)}, u32[]{:S(2)}, u32[]{:S(2)}) async-start(bf16[128,2,2048]{2,1,0:T(2,128)(2,1)} %broadcast_select_fusion.3), calls=%async_computation.8 | async-start | bytes 2097152 | tf_op jit(solution)/shard_map/all_to_all | solution.py:106
  324.0 55.1 %all-to-all-done.8 = bf16[128,2,2048]{2,1,0:T(2,128)(2,1)} async-done(((bf16[128,2,2048]{2,1,0:T(2,128)(2,1)}), bf16[128,2,2048]{2,1,0:T(2,128)(2,1)}, u32[]{:S(2)}, u32[]{:S(2)}) %all-to-all-start.8) | async-done | bytes 1048608 | tf_op jit(solution)/shard_map/all_to_all | solution.py:106
  (145 shorter events, 53.2 us)
Async XLA Ops:
  1.8 53.7 %copy-start = (bf16[2,2,1024,256]{3,2,1,0:T(8,128)(2,1)S(1)}, bf16[2,2,1024,256]{3,2,1,0:T(8,128)(2,1)}, u32[]{:S(2)}) copy-start(bf16[2,2,1024,256]{3,2,1,0:T(8,128)(2,1)} %param.7) | copy-start | bytes 6291460
  2.6 11.5 %all-to-all-start = ((f32[4,2,64,256]{3,2,1,0:T(8,128)}), f32[4,2,64,256]{3,2,1,0:T(8,128)S(1)}, u32[]{:S(2)}, u32[]{:S(2)}) async-start(f32[4,2,64,256]{3,2,1,0:T(8,128)} %stack.21), calls=%async_computation | async-start | bytes 1048576 | tf_op jit(solution)/shard_map/all_to_all | solution.py:12
  7.0 42.1 %copy-start.22 = (s32[1,2,64]{2,1,0:T(2,128)}, s32[1,2,64]{2,1,0:T(2,128)S(1)}, u32[]{:S(2)}) copy-start(s32[1,2,64]{2,1,0:T(2,128)S(1)} %get-tuple-element.16) | copy-start | bytes 1540
  14.1 35.0 %all-to-all-start.1 = ((s32[128,1,2]{2,1,0:T(1,128)}), s32[128,1,2]{2,1,0:T(1,128)S(1)}, u32[]{:S(2)}, u32[]{:S(2)}) async-start(s32[128,1,2]{2,1,0:T(1,128)} %bitcast.4), calls=%async_computation.1 | async-start | bytes 131072 | tf_op jit(solution)/shard_map/all_to_all | solution.py:76
  37.3 18.7 %copy-start.5 = (f32[2,256,128]{2,1,0:T(8,128)}, f32[2,256,128]{2,1,0:T(8,128)S(1)}, u32[]{:S(2)}) copy-start(f32[2,256,128]{2,1,0:T(8,128)S(1)} %fusion.13) | copy-start | bytes 786436
  49.1 44.1 %copy-start.9 = (s32[128,1,2]{2,1,0:T(1,128)}, s32[128,1,2]{2,1,0:T(1,128)S(1)}, u32[]{:S(2)}) copy-start(s32[128,1,2]{2,1,0:T(1,128)S(1)} %all-to-all-done.1) | copy-start | bytes 3076
  49.1 20.7 %all-to-all-start.4 = ((s32[128,1,2]{2,1,0:T(1,128)}), s32[128,1,2]{2,1,0:T(1,128)S(1)}, u32[]{:S(2)}, u32[]{:S(2)}) async-start(s32[128,1,2]{2,1,0:T(1,128)} %bitcast.12), calls=%async_computation.4 | async-start | bytes 131072 | tf_op jit(solution)/shard_map/all_to_all | solution.py:76
  59.0 10.8 %copy-start.14 = (f32[2,64,256]{2,1,0:T(8,128)S(1)}, f32[2,64,256]{2,1,0:T(8,128)}, u32[]{:S(2)}) copy-start(f32[2,64,256]{2,1,0:T(8,128)} %get-tuple-element.15) | copy-start | bytes 393220
  69.8 23.5 %copy-start.11 = (s32[128,1,2]{2,1,0:T(1,128)}, s32[128,1,2]{2,1,0:T(1,128)S(1)}, u32[]{:S(2)}) copy-start(s32[128,1,2]{2,1,0:T(1,128)S(1)} %all-to-all-done.4) | copy-start | bytes 3076
  70.6 13.3 %all-to-all-start.3 = ((f32[4,2,64,256]{3,2,1,0:T(8,128)}), f32[4,2,64,256]{3,2,1,0:T(8,128)}, u32[]{:S(2)}, u32[]{:S(2)}) async-start(f32[4,2,64,256]{3,2,1,0:T(8,128)} %stack.22), calls=%async_computation.3 | async-start | bytes 1048576 | tf_op jit(solution)/shard_map/all_to_all | solution.py:12
  75.9 16.6 %copy-start.17 = (s32[256]{0:T(256)S(1)}, s32[256]{0:T(256)}, u32[]{:S(2)}) copy-start(s32[256]{0:T(256)} %get-tuple-element.10) | copy-start | bytes 3076
  77.9 69.9 %copy-start.13 = (f32[2,64,256]{2,1,0:T(8,128)S(1)}, f32[2,64,256]{2,1,0:T(8,128)}, u32[]{:S(2)}) copy-start(f32[2,64,256]{2,1,0:T(8,128)} %get-tuple-element.14) | copy-start | bytes 393220
  83.9 63.9 %all-to-all-start.2 = ((bf16[128,2,2048]{2,1,0:T(2,128)(2,1)}), bf16[128,2,2048]{2,1,0:T(2,128)(2,1)}, u32[]{:S(2)}, u32[]{:S(2)}) async-start(bf16[128,2,2048]{2,1,0:T(2,128)(2,1)} %broadcast_select_fusion.2), calls=%async_computation.2 | async-start | bytes 2097152 | tf_op jit(solution)/shard_map/all_to_all | solution.py:75
  96.3 61.5 %copy-start.3 = (f32[2,4,64,256]{3,2,1,0:T(8,128)}, f32[2,4,64,256]{3,2,1,0:T(8,128)S(1)}, u32[]{:S(2)}) copy-start(f32[2,4,64,256]{3,2,1,0:T(8,128)S(1)} %copy.62) | copy-start | bytes 1572868
  148.6 18.1 %all-to-all-start.6 = ((f32[4,2,64,256]{3,2,1,0:T(8,128)}), f32[4,2,64,256]{3,2,1,0:T(8,128)}, u32[]{:S(2)}, u32[]{:S(2)}) async-start(f32[4,2,64,256]{3,2,1,0:T(8,128)} %stack.23), calls=%async_computation.6 | async-start | bytes 1048576 | tf_op jit(solution)/shard_map/all_to_all | solution.py:12
  166.7 62.6 %all-to-all-start.5 = ((bf16[128,2,2048]{2,1,0:T(2,128)(2,1)}), bf16[128,2,2048]{2,1,0:T(2,128)(2,1)}, u32[]{:S(2)}, u32[]{:S(2)}) async-start(bf16[128,2,2048]{2,1,0:T(2,128)(2,1)} %broadcast_select_fusion), calls=%async_computation.5 | async-start | bytes 2097152 | tf_op jit(solution)/shard_map/all_to_all | solution.py:75
  239.1 10.2 %copy-start.23 = (s32[1,2,64]{2,1,0:T(2,128)S(1)}, s32[1,2,64]{2,1,0:T(2,128)}, u32[]{:S(2)}) copy-start(s32[1,2,64]{2,1,0:T(2,128)} %copy-done.22) | copy-start | bytes 1540
  239.1 10.3 %copy-start.27 = (s32[128]{0:T(128)S(1)}, s32[128]{0:T(128)}, u32[]{:S(2)}) copy-start(s32[128]{0:T(128)} %copy-done.26) | copy-start | bytes 1540
  239.1 10.3 %copy-start.15 = (s32[128,2]{1,0:T(8,128)S(1)}, s32[128,2]{1,0:T(8,128)}, u32[]{:S(2)}) copy-start(s32[128,2]{1,0:T(8,128)} %get-tuple-element.5) | copy-start | bytes 3076
  239.1 10.5 %copy-start.10 = (s32[128,1,2]{2,1,0:T(1,128)S(1)}, s32[128,1,2]{2,1,0:T(1,128)}, u32[]{:S(2)}) copy-start(s32[128,1,2]{2,1,0:T(1,128)} %copy-done.9) | copy-start | bytes 3076
  242.3 62.2 %all-to-all-start.7 = ((bf16[128,2,2048]{2,1,0:T(2,128)(2,1)}), bf16[128,2,2048]{2,1,0:T(2,128)(2,1)}, u32[]{:S(2)}, u32[]{:S(2)}) async-start(bf16[128,2,2048]{2,1,0:T(2,128)(2,1)} %broadcast_select_fusion.1), calls=%async_computation.7 | async-start | bytes 2097152 | tf_op jit(solution)/shard_map/all_to_all | solution.py:106
  313.8 10.2 %copy-start.21 = (s32[1,2,64]{2,1,0:T(2,128)S(1)}, s32[1,2,64]{2,1,0:T(2,128)}, u32[]{:S(2)}) copy-start(s32[1,2,64]{2,1,0:T(2,128)} %copy-done.20) | copy-start | bytes 1540
  313.8 10.3 %copy-start.25 = (s32[128]{0:T(128)S(1)}, s32[128]{0:T(128)}, u32[]{:S(2)}) copy-start(s32[128]{0:T(128)} %copy-done.24) | copy-start | bytes 1540
  317.0 62.2 %all-to-all-start.8 = ((bf16[128,2,2048]{2,1,0:T(2,128)(2,1)}), bf16[128,2,2048]{2,1,0:T(2,128)(2,1)}, u32[]{:S(2)}, u32[]{:S(2)}) async-start(bf16[128,2,2048]{2,1,0:T(2,128)(2,1)} %broadcast_select_fusion.3), calls=%async_computation.8 | async-start | bytes 2097152 | tf_op jit(solution)/shard_map/all_to_all | solution.py:106
  (13 other events, 42.7 us)
